TPU v7x, 256 devices: a whole 4x4x8 slice. The times are simulated.
256 devices in a mesh: group: 4 (over y), resp: 16 (over z, core), tp: 4 (over x).
Axes of the slice: x: 4, y: 4, z: 8, core: 2. Of those that a mesh axis runs over, the one named last changes fastest.
Arguments:
- query: bfloat16 [16384, 4096], P(('group', 'resp'), 'tp'), parts along dimension 0, may hold values from -150 to 150
- resp_kv: bfloat16 [16384, 2, 1024], P(('group', 'resp'), None, 'tp'), parts along dimension 0, may hold values from -6 to 6
- prefix_kv: bfloat16 [4096, 2, 1024], P(('group', 'resp'), None, 'tp'), parts along dimension 0, may hold values from -6 to 6
- ssm_x: bfloat16 [16384, 8192], P(('group', 'resp'), 'tp'), parts along dimension 0, may hold values from -6 to 6
- bc: bfloat16 [16384, 2, 256], P(('group', 'resp')), parts along dimension 0, may hold values from -1.5 to 1.5
- step_size: float32 [256, 4096], P(('group', 'tp'), 'resp'), parts along dimension 0, may hold values from 0 to 1
- prefix_state: float32 [64, 64, 128, 256], P(('group', 'resp'), 'tp'), parts along dimension 0, may hold values from -1.5 to 1.5
- owner: int32 [256], P(('group', 'tp')), parts along dimension 0, may hold values from 0 to 15
- lengths: int32 [64], P(('group', 'resp')), parts along dimension 0, may hold values from 64 to 256, as said below
- advantage: float32 [64], P(('group', 'resp')), parts along dimension 0, may hold values from -3 to 3
- grad_attn: bfloat16 [16384, 4096], P(('group', 'resp'), 'tp'), parts along dimension 0, may hold values from -6 to 6
- grad_ssm: bfloat16 [16384, 8192], P(('group', 'resp'), 'tp'), parts along dimension 0, may hold values from -6 to 6
Outputs:
- attn_out: bfloat16 [16384, 4096], P(('group', 'resp'), 'tp'), parts along dimension 0
- ssm_out: bfloat16 [16384, 8192], P(('group', 'resp'), 'tp'), parts along dimension 0
- grad_query: bfloat16 [16384, 4096], P(('group', 'resp'), 'tp'), parts along dimension 0
- grad_prefix_kv: bfloat16 [4096, 2, 1024], P(('group', 'resp'), None, 'tp'), parts along dimension 0
- grad_bc: bfloat16 [16384, 2, 256], P(('group', 'resp', 'tp')), parts along dimension 0
- grad_state: float32 [256, 128, 256], P(('group', 'tp')), parts along dimension 0
There are 4 independent parts, one for each index of `group`. A program takes and returns all parts, laid end to end along the dimension named above; each array names one. Nothing has to cross between parts.
Inputs may be any that keep to these rules, and one draw needn't show every extreme that they name: `lengths`: one response of each group has exactly 256 live tokens.
All inputs are finite; a program needn't handle non-finite values.
Results may differ from a plain program's by a relative error of at most 0.025.
Values may be sent and summed in bfloat16 or wider, within the bound.
No kernel may reach another device: no remote copies, remote signals or barrier semaphores. Data moves between devices by JAX's collectives and lax.ppermute only.
A program may use at most 128 MiB of HBM per device.

v0:
```python
import math
import jax
import jax.numpy as jnp
from jax import lax
from jax.sharding import PartitionSpec as P

HEAD_DIM = 128
SSM_DIM = 128
highest = lax.Precision.HIGHEST


def on_device(
    query,
    resp_kv,
    prefix_kv,
    ssm_x,
    bc,
    step_size,
    prefix_state,
    owner,
    lengths,
    advantage,
    grad_attn,
    grad_ssm,
):
    steps_len = query.shape[0]
    kv_local = resp_kv.shape[2] // HEAD_DIM
    group_size = query.shape[1] // resp_kv.shape[2]
    inv_scale = 1.0 / math.sqrt(HEAD_DIM)
    positions = jnp.arange(steps_len)
    causal = positions[None, :] <= positions[:, None]
    factor = advantage[0] * steps_len / lengths[0].astype(jnp.float32)
    alive_rows = (positions < lengths[0]).astype(jnp.float32) * factor
    grad_out = (alive_rows[:, None] * grad_attn.astype(jnp.float32)).astype(jnp.bfloat16)
    grad_y = (alive_rows[:, None] * grad_ssm.astype(jnp.float32)).astype(jnp.bfloat16)
    cache = lax.all_gather(prefix_kv, "resp", axis=0, tiled=True)
    prefix_count = cache.shape[0]
    query_heads = query.reshape(steps_len, kv_local, group_size, HEAD_DIM)
    grad_heads = grad_out.reshape(steps_len, kv_local, group_size, HEAD_DIM)
    prefix_keys = cache[:, 0].reshape(prefix_count, kv_local, HEAD_DIM)
    prefix_values = cache[:, 1].reshape(prefix_count, kv_local, HEAD_DIM)
    own_keys = resp_kv[:, 0].reshape(steps_len, kv_local, HEAD_DIM)
    own_values = resp_kv[:, 1].reshape(steps_len, kv_local, HEAD_DIM)
    prefix_scores = (
        jnp.einsum("tgid,kgd->gitk", query_heads, prefix_keys, preferred_element_type=jnp.float32)
        * inv_scale
    )
    own_scores = jnp.where(
        causal,
        jnp.einsum("tgid,kgd->gitk", query_heads, own_keys, preferred_element_type=jnp.float32)
        * inv_scale,
        -jnp.inf,
    )
    row_top = jnp.maximum(jnp.max(prefix_scores, -1), jnp.max(own_scores, -1))
    row_total = jnp.sum(jnp.exp(prefix_scores - row_top[..., None]), -1) + jnp.sum(
        jnp.exp(own_scores - row_top[..., None]), -1
    )
    log_total = row_top + jnp.log(row_total)
    prefix_weights = jnp.exp(prefix_scores - log_total[..., None]).astype(jnp.bfloat16)
    own_weights = jnp.exp(own_scores - log_total[..., None]).astype(jnp.bfloat16)
    attended = jnp.einsum(
        "gitk,kgd->tgid", prefix_weights, prefix_values, preferred_element_type=jnp.float32
    ) + jnp.einsum("gitk,kgd->tgid", own_weights, own_values, preferred_element_type=jnp.float32)
    attn_out = attended.reshape(steps_len, -1).astype(jnp.bfloat16)
    row_delta = jnp.transpose(jnp.sum(grad_heads.astype(jnp.float32) * attended, -1), (1, 2, 0))
    prefix_slope = jnp.einsum(
        "tgid,kgd->gitk", grad_heads, prefix_values, preferred_element_type=jnp.float32
    )
    own_slope = jnp.einsum(
        "tgid,kgd->gitk", grad_heads, own_values, preferred_element_type=jnp.float32
    )
    prefix_score_grad = (
        prefix_weights.astype(jnp.float32) * (prefix_slope - row_delta[..., None]) * inv_scale
    ).astype(jnp.bfloat16)
    own_score_grad = (
        own_weights.astype(jnp.float32) * (own_slope - row_delta[..., None]) * inv_scale
    ).astype(jnp.bfloat16)
    grad_query = (
        (
            jnp.einsum(
                "gitk,kgd->tgid", prefix_score_grad, prefix_keys, preferred_element_type=jnp.float32
            )
            + jnp.einsum(
                "gitk,kgd->tgid", own_score_grad, own_keys, preferred_element_type=jnp.float32
            )
        )
        .reshape(steps_len, -1)
        .astype(jnp.bfloat16)
    )
    block_rows = prefix_kv.shape[0]
    grad_keys = jnp.einsum(
        "gitk,tgid->kgd", prefix_score_grad, query_heads, preferred_element_type=jnp.float32
    )
    grad_values = jnp.einsum(
        "gitk,tgid->kgd", prefix_weights, grad_heads, preferred_element_type=jnp.float32
    )
    grad_prefix_kv = lax.psum_scatter(
        jnp.stack(
            [
                grad_keys.reshape(lax.axis_size("resp") * block_rows, -1),
                grad_values.reshape(lax.axis_size("resp") * block_rows, -1),
            ],
            axis=1,
        ).astype(jnp.bfloat16),
        "resp",
        scatter_dimension=0,
        tiled=True,
    )
    heads_local = step_size.shape[0]
    head_inputs = ssm_x.reshape(steps_len, heads_local, SSM_DIM)
    input_maps = bc[:, 0]
    read_maps = bc[:, 1]
    read_wide = read_maps.astype(jnp.float32)
    cumulative = jnp.cumsum(step_size, axis=1)
    segment = jnp.exp(
        jnp.where(causal[None], cumulative[:, None, :] - cumulative[:, :, None], -jnp.inf)
    )
    pair_inner = jnp.dot(read_maps, input_maps.T, preferred_element_type=jnp.float32)
    mixing = (segment * step_size[:, None, :] * pair_inner[None]).astype(jnp.bfloat16)
    from_inputs = jnp.einsum(
        "hts,shp->thp", mixing, head_inputs, preferred_element_type=jnp.float32
    )
    held_here = (owner == lax.axis_index("resp"))[:, None, None]
    own_slot = jnp.where(held_here, prefix_state[0], jnp.zeros_like(prefix_state[0]))
    start_state = lax.psum(own_slot.astype(jnp.bfloat16), "resp").astype(jnp.float32)
    carried = jnp.exp(-cumulative)
    from_state = (
        jnp.einsum("tn,hpn->thp", read_wide, start_state, precision=highest) * carried.T[:, :, None]
    )
    ssm_out = (from_inputs + from_state).reshape(steps_len, -1).astype(jnp.bfloat16)
    grad_heads_y = grad_y.reshape(steps_len, heads_local, SSM_DIM)
    inner_grad = jnp.einsum(
        "thp,shp->hts", grad_heads_y, head_inputs, preferred_element_type=jnp.float32
    )
    grad_mix = (segment * step_size[:, None, :] * inner_grad).astype(jnp.bfloat16)
    weighted = grad_heads_y.astype(jnp.float32) * carried.T[:, :, None]
    grad_read = jnp.einsum(
        "hts,sn->tn", grad_mix, input_maps, preferred_element_type=jnp.float32
    ) + jnp.einsum("thp,hpn->tn", weighted, start_state, precision=highest)
    grad_input = jnp.einsum("hts,tn->sn", grad_mix, read_maps, preferred_element_type=jnp.float32)
    state_term = jnp.einsum("thp,tn->hpn", weighted, read_wide, precision=highest)
    grad_state = lax.psum(state_term.astype(jnp.bfloat16), "resp").astype(jnp.float32)
    map_terms = jnp.stack([grad_input, grad_read], axis=1)
    whole_sum = lax.psum(map_terms.astype(jnp.bfloat16), "tp").astype(jnp.float32)
    share_rows = steps_len // lax.axis_size("tp")
    grad_bc = lax.dynamic_slice_in_dim(
        whole_sum, lax.axis_index("tp") * share_rows, share_rows, 0
    ).astype(jnp.bfloat16)
    return (attn_out, ssm_out, grad_query, grad_prefix_kv, grad_bc, grad_state)


def solution(mesh):
    return jax.shard_map(
        on_device,
        mesh=mesh,
        in_specs=(
            P(("group", "resp"), "tp"),
            P(("group", "resp"), None, "tp"),
            P(("group", "resp"), None, "tp"),
            P(("group", "resp"), "tp"),
            P(("group", "resp"), None, None),
            P(("group", "tp"), "resp"),
            P(("group", "resp"), "tp", None, None),
            P(("group", "tp")),
            P(("group", "resp")),
            P(("group", "resp")),
            P(("group", "resp"), "tp"),
            P(("group", "resp"), "tp"),
        ),
        out_specs=(
            P(("group", "resp"), "tp"),
            P(("group", "resp"), "tp"),
            P(("group", "resp"), "tp"),
            P(("group", "resp"), None, "tp"),
            P(("group", "resp", "tp"), None, None),
            P(("group", "tp"), None, None),
        ),
        check_vma=False,
    )
```

profile of v0, /device:TPU:8, one launch (start us, length us, event | category | flops | bytes accessed | tf_op | source)
XLA Modules:
  0.0 269.7 jit_solution(11355581099030665395)
XLA Ops:
  7.2 0.0 all-gather.2.cloned.1.call-start
  7.2 0.7 all-gather.2.cloned.1.call-update
  7.9 0.0 all-reduce.7.cloned.1.call-start
  9.3 0.7 copy_bitcast_fusion.4
  10.0 0.6 reduce-window.6
  10.5 0.2 slice_reduce_fusion
  10.8 0.1 exponential_bitcast_fusion
  10.8 0.2 mul.110
  11.0 1.8 copy.121
  12.9 3.2 %convert_multiply_fusion = (f32[256,2048]{1,0:T(8,128)S(1)}, bf16[256,2048]{1,0:T(8,128)(2,1)}) fusion(f32[256,2048]{1,0:T(8,128)} %copy.121, bf16[256,2048]{1,0:T(8,128)(2,1)} %param.23, f32[256]{0:T(256)S(1)} %compare_select_fusion), kind=kLoop, calls=%fused_computation.26 | loop fusion | flops 2621440 | bytes 6292480 | tf_op jit(solution)/shard_map/mul | solution.py:136
  16.1 1.2 fusion.53
  17.2 1.1 copy.159
  18.3 2.0 copy.162
  20.3 2.0 multiply_convert_fusion.4
  22.3 2.0 copy.103
  24.4 1.1 copy.95
  25.4 1.8 copy.157
  27.3 2.3 fusion.52
  29.6 1.3 copy.117
  30.9 0.8 copy.97
  31.7 0.7 copy_bitcast_fusion.3
  32.4 1.5 fusion.54
  34.0 1.3 fusion.13
  35.3 0.7 copy-done.5
  35.9 2.1 convolution_convert_fusion
  38.0 13.4 %all-gather.2.cloned.1.call-done = bf16[1024,2,256]{2,1,0:T(2,128)(2,1)} async-done(((bf16[64,2,256]{2,1,0:T(2,128)(2,1)}), bf16[1024,2,256]{2,1,0:T(2,128)(2,1)}) %all-gather.2.cloned.1.call-update) | async-done | bytes 1048592 | tf_op jit(solution)/shard_map/all_gather | solution.py:36
  51.4 4.3 %fusion.51 = (bf16[1024,1,256]{2,1,0:T(2,128)(2,1)}, bf16[1024,1,256]{2,1,0:T(2,128)(2,1)}) fusion(bf16[1024,2,256]{2,1,0:T(2,128)(2,1)} %all-gather.2.cloned.1.call-done), kind=kLoop, calls=%fused_computation.85 | loop fusion | bytes 2097152 | tf_op jit(solution)/shard_map/slice | solution.py:40
  55.7 3.5 %copy.158 = bf16[1024,1,256]{0,2,1:T(8,128)(2,1)} copy(bf16[1024,1,256]{2,1,0:T(2,128)(2,1)} %get-tuple-element.31) | data formatting | bytes 1048576
  59.2 2.5 bitcast_reduce_fusion
  61.8 0.3 exponential_reduce_fusion
  62.1 1.4 fusion.4
  63.5 3.4 %fusion.6 = bf16[2,4,256,1024]{2,3,1,0:T(8,128)(2,1)} fusion(f32[2,1024,256,4]{2,1,3,0:T(8,128)S(1)} %get-tuple-element.38, f32[2,4,256]{2,1,0:T(4,128)S(1)} %bitcast.215), kind=kLoop, calls=%fused_computation.10 | loop fusion | flops 6291456 | bytes 12591104 | tf_op jit(solution)/shard_map/convert_element_type | solution.py:59
  66.8 3.5 %copy.93 = bf16[1024,1,256]{0,2,1:T(8,128)(2,1)} copy(bf16[1024,1,256]{2,1,0:T(2,128)(2,1)} %get-tuple-element.32) | data formatting | bytes 1048576 | tf_op jit(solution)/shard_map/slice | solution.py:41
  70.3 3.2 %fusion.55 = f32[2,4,256,128]{2,3,1,0:T(8,128)S(1)} fusion(bf16[1024,2,128,1]{0,2,3,1:T(8,128)(2,1)} %bitcast.202, bf16[2,4,256,1024]{2,3,1,0:T(8,128)(2,1)} %fusion.6), kind=kOutput, calls=%fused_computation.89 | convolution fusion | flops 536870912 | bytes 5767168 | tf_op jit(solution)/shard_map/gitk,kgd->tgid/dot_general | solution.py:61
  73.5 0.4 copy-done.1
  73.9 0.1 copy-done.4
  74.0 2.3 fusion.28
  76.4 1.3 multiply_reduce_fusion
  77.7 1.8 fusion.2
  79.5 2.3 fusion.27
  81.8 3.6 %copy.115 = bf16[1024,1,256]{2,1,0:T(2,128)(2,1)} copy(bf16[1024,1,256]{0,2,1:T(8,128)(2,1)} %bitcast.206) | data formatting | bytes 1048576 | tf_op jit(solution)/shard_map/stack;reshape | solution.py:98
  85.3 3.6 %copy.116 = bf16[1024,1,256]{2,1,0:T(2,128)(2,1)} copy(bf16[1024,1,256]{0,2,1:T(8,128)(2,1)} %bitcast.205) | data formatting | bytes 1048576 | tf_op jit(solution)/shard_map/stack;reshape | solution.py:98
  88.9 4.2 %pad_maximum_fusion = bf16[1024,2,256]{2,1,0:T(2,128)(2,1)} fusion(bf16[1024,1,256]{2,1,0:T(2,128)(2,1)} %copy.116, bf16[1024,1,256]{2,1,0:T(2,128)(2,1)} %copy.115), kind=kLoop, calls=%fused_computation.57 | loop fusion | flops 2097152 | bytes 2097152 | tf_op jit(solution)/shard_map/stack | solution.py:98
  93.1 0.0 all-reduce.5.cloned.1.call-start
  93.2 3.4 %convert_reduce_fusion = bf16[256,256]{1,0:T(8,128)(2,1)} fusion(bf16[256,16,128]{0,2,1:T(8,128)(2,1)} %bitcast.213, f32[16,256]{1,0:T(8,128)} %param.17, f32[16,256]{1,0:T(8,128)} %copy_bitcast_fusion.3, pred[256,256]{1,0:T(8,128)(4,1)} %copy.97, bf16[256,2048]{1,0:T(8,128)(2,1)S(1)} %copy-done), kind=kOutput, calls=%fused_computation.11 | convolution fusion | flops 275709952 | bytes 2326528 | tf_op jit(solution)/shard_map/thp,shp->hts/dot_general | solution.py:132
  96.6 1.3 dynamic-slice
  98.5 1.8 fusion.33
  100.3 1.2 fusion.47
  101.5 4.1 %fusion.7 = f32[16,256,128]{1,2,0:T(8,128)} fusion(f32[256,256]{1,0:T(8,128)S(1)} %fusion.47, f32[16,256]{1,0:T(8,128)} %param.17, f32[16,256]{1,0:T(8,128)} %copy_bitcast_fusion.3, pred[256,256]{1,0:T(8,128)(4,1)} %copy.97, bf16[256,2048]{1,0:T(8,128)(2,1)S(1)} %copy-done), kind=kOutput, calls=%fused_computation.15 | convolution fusion | flops 273678336 | bytes 3506176 | tf_op jit(solution)/shard_map/hts,shp->thp/dot_general | solution.py:120
  105.6 1.7 fusion.56
  107.3 3.1 %fusion.26 = bf16[2,4,256,128]{2,3,1,0:T(8,128)(2,1)} fusion(f32[2,4,256,128]{2,3,1,0:T(8,128)} %fusion.56, bf16[256,2,128,1]{0,2,3,1:T(8,128)(2,1)S(1)} %bitcast.210, bf16[256,2,4,128]{0,3,2,1:T(8,128)(2,1)} %bitcast.192, bf16[256,2,128,1]{0,2,3,1:T(8,128)(2,1)S(1)} %bitcast.212, f32[2,4,256]{2,1,0:T(4,128)S(1)} %bitcast.220, ...), kind=kOutput, calls=%fused_computation.46 | convolution fusion | flops 272629760 | bytes 4472832 | tf_op jit(solution)/shard_map/gitk,kgd->tgid/dot_general | solution.py:83
  110.4 2.2 copy.125
  112.5 2.1 copy.123
  114.6 96.1 %all-reduce.7.cloned.1.call-done = (bf16[16,128,256]{2,1,0:T(8,128)(2,1)}, bf16[1024,2,256]{2,1,0:T(2,128)(2,1)}, bf16[16,128,256]{2,1,0:T(8,128)(2,1)}) async-done(((bf16[16,128,256]{2,1,0:T(8,128)(2,1)}, bf16[1024,2,256]{2,1,0:T(2,128)(2,1)}, bf16[16,128,256]{2,1,0:T(8,128)(2,1)}), (bf16[16,128,256]{2,1,0:T(8,128)(2,1)}, bf16[1024,2,256]{2,1,0:T(2,128)(2,1)}, ...) | async-done | bytes 3145744 | tf_op jit(solution)/shard_map/psum | solution.py:125
  210.7 3.0 %fusion.29 = f32[256,256]{1,0:T(8,128)S(1)} fusion(bf16[16,128,256]{2,1,0:T(8,128)(2,1)} %get-tuple-element.24, bf16[256,16,128]{0,2,1:T(8,128)(2,1)S(1)} %bitcast.214, f32[256,16]{0,1:T(8,128)S(1)} %copy-done.19), kind=kOutput, calls=%fused_computation.50 | convolution fusion | flops 1611661312 | bytes 2375680 | tf_op jit(solution)/shard_map/thp,hpn->tn/dot_general | solution.py:139
  213.8 0.2 fusion.34
  214.0 0.7 pad_maximum_fusion.1
  214.8 2.5 fusion.12
  217.2 1.5 convert_element_type.121
  218.8 1.4 copy.124
  220.2 1.5 constant_dynamic-slice_fusion
  221.7 39.9 %all-reduce.5.cloned.1.call-done = bf16[256,2,256]{2,0,1:T(8,128)(2,1)} async-done(((bf16[256,2,256]{2,0,1:T(8,128)(2,1)}), bf16[256,2,256]{2,0,1:T(8,128)(2,1)}) %all-reduce.5.cloned.1.call-update) | async-done | bytes 262160 | tf_op jit(solution)/shard_map/psum | solution.py:144
  261.6 0.8 convert_convert_fusion
  262.4 0.7 copy.126
  (53 shorter events, 0.2 us)
Async XLA Ops:
  7.2 86.0 %copy-start = (bf16[256,2048]{1,0:T(8,128)(2,1)S(1)}, bf16[256,2048]{1,0:T(8,128)(2,1)}, u32[]{:S(2)}) copy-start(bf16[256,2048]{1,0:T(8,128)(2,1)} %param.15) | copy-start | bytes 3145732
  7.2 44.2 %all-gather.2.cloned.1.call-start = ((), (), s32[]{:S(2)}) async-start(), calls=%async_computation | async-start | bytes 1114112 | tf_op jit(solution)/shard_map/all_gather | solution.py:36
  7.9 202.8 %all-reduce.7.cloned.1.call-start = ((), (), s32[]{:S(2)}) async-start(), calls=%async_computation.2 | async-start | bytes 6291456 | tf_op jit(solution)/shard_map/psum | solution.py:125
  10.7 2.1 copy-start.20
  10.8 2.0 copy-start.18
  12.9 3.2 %copy-start.13 = (bf16[256,2,256]{2,1,0:T(2,128)(2,1)S(1)}, bf16[256,2,256]{2,1,0:T(2,128)(2,1)}, u32[]{:S(2)}) copy-start(bf16[256,2,256]{2,1,0:T(2,128)(2,1)} %param.13) | copy-start | bytes 786436
  27.3 2.3 copy-start.9
  27.3 4.5 %copy-start.22 = (s32[16]{0:T(128)S(1)}, s32[16]{0:T(128)}, u32[]{:S(2)}) copy-start(s32[16]{0:T(128)} %param.19) | copy-start | bytes 196
  27.3 4.5 %copy-start.21 = (f32[16,2]{0,1:T(2,128)S(1)}, f32[16,2]{0,1:T(2,128)}, u32[]{:S(2)}) copy-start(f32[16,2]{0,1:T(2,128)} %copy-done.20) | copy-start | bytes 388
  30.9 1.5 copy-start.15
  31.7 2.3 copy-start.10
  34.0 2.0 copy-start.5
  70.3 3.6 %copy-start.1 = (bf16[2,4,256,1024]{2,3,1,0:T(8,128)(2,1)S(1)}, bf16[2,4,256,1024]{2,3,1,0:T(8,128)(2,1)}, u32[]{:S(2)}) copy-start(bf16[2,4,256,1024]{2,3,1,0:T(8,128)(2,1)} %fusion.6) | copy-start | bytes 12582916
  70.3 3.7 %copy-start.4 = (bf16[256,1024]{0,1:T(8,128)(2,1)S(1)}, bf16[256,1024]{0,1:T(8,128)(2,1)}, u32[]{:S(2)}) copy-start(bf16[256,1024]{0,1:T(8,128)(2,1)} %copy.103) | copy-start | bytes 1572868
  76.4 1.3 copy-start.8
  77.7 1.8 copy-start.6
  79.5 2.3 copy-start.2
  93.1 168.5 %all-reduce.5.cloned.1.call-start = ((), (), s32[]{:S(2)}) async-start(), calls=%async_computation.1 | async-start | bytes 524288 | tf_op jit(solution)/shard_map/psum | solution.py:144
  101.5 4.1 %copy-start.3 = (bf16[2,4,256,1024]{2,3,1,0:T(8,128)(2,1)S(1)}, bf16[2,4,256,1024]{2,3,1,0:T(8,128)(2,1)}, u32[]{:S(2)}) copy-start(bf16[2,4,256,1024]{2,3,1,0:T(8,128)(2,1)} %copy-done.2) | copy-start | bytes 12582916
  101.5 4.1 %copy-start.7 = (bf16[1024,1,256]{0,2,1:T(8,128)(2,1)S(1)}, bf16[1024,1,256]{0,2,1:T(8,128)(2,1)}, u32[]{:S(2)}) copy-start(bf16[1024,1,256]{0,2,1:T(8,128)(2,1)} %copy.158) | copy-start | bytes 1572868
  110.4 100.3 %copy-start.12 = (bf16[256,2048]{0,1:T(8,128)(2,1)S(1)}, bf16[256,2048]{0,1:T(8,128)(2,1)}, u32[]{:S(2)}) copy-start(bf16[256,2048]{0,1:T(8,128)(2,1)} %copy.117) | copy-start | bytes 3145732
  110.4 100.3 %copy-start.19 = (f32[256,16]{0,1:T(8,128)S(1)}, f32[256,16]{0,1:T(8,128)}, u32[]{:S(2)}) copy-start(f32[256,16]{0,1:T(8,128)} %copy-done.18) | copy-start | bytes 49156
  110.4 103.4 %copy-start.14 = (bf16[256,1,256]{2,1,0:T(2,128)(2,1)S(1)}, bf16[256,1,256]{2,1,0:T(2,128)(2,1)}, u32[]{:S(2)}) copy-start(bf16[256,1,256]{2,1,0:T(2,128)(2,1)} %get-tuple-element.33) | copy-start | bytes 393220
  110.4 103.4 %copy-start.16 = (bf16[256,256]{1,0:T(8,128)(2,1)S(1)}, bf16[256,256]{1,0:T(8,128)(2,1)}, u32[]{:S(2)}) copy-start(bf16[256,256]{1,0:T(8,128)(2,1)} %convert_reduce_fusion) | copy-start | bytes 393220
  112.5 101.4 %copy-start.17 = (bf16[256,1,256]{2,0,1:T(8,128)(2,1)S(1)}, bf16[256,1,256]{2,0,1:T(8,128)(2,1)}, u32[]{:S(2)}) copy-start(bf16[256,1,256]{2,0,1:T(8,128)(2,1)} %fusion.33) | copy-start | bytes 393220
  214.7 2.5 copy-start.11
Sparse Core Ops, SparseCore 0:
  9.8 41.4 all-gather.1
  93.2 117.4 all-reduce.6
  214.9 46.6 all-reduce.4
where the time goes:
time: 271 us; the launch traced here: 270 us
  waiting for transfers between devices  150 us (55%)
  local copies, waits for them, and re-layouts  45.2 us (17%)
  matrix products  38 us (14%)
  other arithmetic  20.2 us (7%)
  between operations  16 us (6%)
    psum x1, waiting for transfers between devices, on_device(): lax.psum(own_slot.astype(jnp.bfloat16), 'resp').astype(jnp.float32)  96.1 us
    psum x1, waiting for transfers between devices, on_device(): lax.psum(map_terms.astype(jnp.bfloat16), 'tp').astype(jnp.float32)  39.9 us
    unnamed x55, local copies, waits for them, and re-layouts  15 us
    all_gather x1, waiting for transfers between devices, on_device(): cache = lax.all_gather(prefix_kv, 'resp', axis=0, tiled=True)  13.4 us
    another operation x2, local copies, waits for them, and re-layouts, on_device(): jnp.stack([grad_keys.reshape(lax.axis_size('resp') * block_rows, -1), gra...  7.11 us
  transfers between devices with their start and end apart: 3, of which 3 were waited for; matrix products, arithmetic and copies ran while one was open for 21% of the time, Pallas kernels for 0%

commit v1 on v0

--- a/solution.py
+++ b/solution.py
@@ -122,7 +122,9 @@
     )
     held_here = (owner == lax.axis_index("resp"))[:, None, None]
     own_slot = jnp.where(held_here, prefix_state[0], jnp.zeros_like(prefix_state[0]))
-    start_state = lax.psum(own_slot.astype(jnp.bfloat16), "resp").astype(jnp.float32)
+    start_state = jnp.sum(lax.all_gather(own_slot.astype(jnp.bfloat16), "resp"), axis=0).astype(
+        jnp.float32
+    )
     carried = jnp.exp(-cumulative)
     from_state = (
         jnp.einsum("tn,hpn->thp", read_wide, start_state, precision=highest) * carried.T[:, :, None]

time: 271 us -> 375 us (1.38)
  waiting for transfers between devices: 150 us -> 244 us
  other arithmetic: 20.2 us -> 30.8 us
  matrix products: 38 us -> 34.1 us
  local copies, waits for them, and re-layouts: 45.2 us -> 49.1 us
    psum x1 -> x0, waiting for transfers between devices: 96.1 us -> none  [on_device(): lax.psum(own_slot.astype(jnp.bfloat16), 'resp').astype(jnp.float32)]
    all_gather x0 -> x1, waiting for transfers between devices: none -> 93.6 us  [on_device(): lax.all_gather(own_slot.astype(jnp.bfloat16), 'resp')]
    unnamed x3 -> x5, waiting for transfers between devices: 0.71 us -> 89.2 us
    reduce_sum x0 -> x1, other arithmetic: none -> 8.93 us  [on_device(): jnp.sum(lax.all_gather(own_slot.astype(jnp.bfloat16), 'resp'), axis=0)]
    all_gather x1, waiting for transfers between devices: 13.4 us -> 18.8 us  [on_device(): cache = lax.all_gather(prefix_kv, 'resp', axis=0, tiled=True)]
    unnamed x55 -> x67, local copies, waits for them, and re-layouts: 15 us -> 17.3 us
  transfers between devices with their start and end apart: 3 -> 4, of which waited for: 3 -> 4; matrix products, arithmetic and copies ran while one was open for 21% -> 15% of each run, Pallas kernels for 0% -> 0%
where the time goes in v1:
time: 375 us; the launch traced here: 374 us
  waiting for transfers between devices  244 us (65%)
  local copies, waits for them, and re-layouts  49.1 us (13%)
  matrix products  34.1 us (9%)
  other arithmetic  30.8 us (8%)
  between operations  16.2 us (4%)
    all_gather x1, waiting for transfers between devices, on_device(): lax.all_gather(own_slot.astype(jnp.bfloat16), 'resp')  93.6 us
    unnamed x5, waiting for transfers between devices  89.2 us
    psum x1, waiting for transfers between devices, on_device(): lax.psum(map_terms.astype(jnp.bfloat16), 'tp').astype(jnp.float32)  42 us
    all_gather x1, waiting for transfers between devices, on_device(): cache = lax.all_gather(prefix_kv, 'resp', axis=0, tiled=True)  18.8 us
    unnamed x67, local copies, waits for them, and re-layouts  17.3 us
    reduce_sum x1, other arithmetic, on_device(): jnp.sum(lax.all_gather(own_slot.astype(jnp.bfloat16), 'resp'), axis=0)  8.93 us
  transfers between devices with their start and end apart: 4, of which 4 were waited for; matrix products, arithmetic and copies ran while one was open for 15% of the time, Pallas kernels for 0%

profile of v1, /device:TPU:8, one launch (start us, length us, event | category | flops | bytes accessed | tf_op | source)
XLA Modules:
  0.0 373.8 jit_solution(206731154105567308)
XLA Ops:
  7.2 0.7 all-gather.3.cloned.1.call-update
  9.3 0.7 copy_bitcast_fusion.4
  10.0 0.6 reduce-window.6
  10.6 0.2 slice_reduce_fusion
  10.8 2.0 copy.162
  12.9 1.2 multiply_convert_fusion.4
  14.1 1.0 copy.103
  15.1 1.5 fusion.52
  16.6 0.1 copy.95
  16.8 0.1 copy.159
  16.9 1.1 fusion.51
  18.0 0.1 exponential_bitcast_fusion
  18.1 1.5 mul.110
  19.6 1.9 copy.121
  21.5 3.2 convert_multiply_fusion
  24.7 2.9 copy.157
  27.7 0.6 copy-done.15
  28.3 2.1 fusion.53
  30.5 2.1 convolution_convert_fusion
  32.6 18.8 %all-gather.3.cloned.1.call-done = bf16[1024,2,256]{2,1,0:T(2,128)(2,1)} async-done(((bf16[64,2,256]{2,1,0:T(2,128)(2,1)}), bf16[1024,2,256]{2,1,0:T(2,128)(2,1)}) %all-gather.3.cloned.1.call-update) | async-done | bytes 1048592 | tf_op jit(solution)/shard_map/all_gather | solution.py:36
  51.4 4.3 %fusion.50 = (bf16[1024,1,256]{2,1,0:T(2,128)(2,1)}, bf16[1024,1,256]{2,1,0:T(2,128)(2,1)}) fusion(bf16[1024,2,256]{2,1,0:T(2,128)(2,1)} %all-gather.3.cloned.1.call-done), kind=kLoop, calls=%fused_computation.84 | loop fusion | bytes 2097152 | tf_op jit(solution)/shard_map/slice | solution.py:40
  55.7 3.5 copy.158
  59.2 3.5 copy.93
  62.7 2.5 bitcast_reduce_fusion
  65.3 0.3 exponential_reduce_fusion
  65.6 1.4 fusion.4
  67.0 1.5 fusion.6
  68.5 1.9 copy-done.1
  70.4 2.3 fusion.27
  72.7 3.6 copy.116
  76.2 3.2 fusion.54
  79.5 1.3 multiply_reduce_fusion
  80.8 1.8 fusion.2
  82.6 1.9 copy-done.3
  84.6 2.3 fusion.26
  86.9 3.6 copy.115
  90.4 4.2 %pad_maximum_fusion = bf16[1024,2,256]{2,1,0:T(2,128)(2,1)} fusion(bf16[1024,1,256]{2,1,0:T(2,128)(2,1)} %copy.116, bf16[1024,1,256]{2,1,0:T(2,128)(2,1)} %copy.115), kind=kLoop, calls=%fused_computation.56 | loop fusion | flops 2097152 | bytes 2097152 | tf_op jit(solution)/shard_map/stack | solution.py:98
  94.7 0.7 broadcast_compare_fusion
  95.3 2.8 select_convert_fusion
  98.3 1.6 copy.97
  99.9 2.3 copy.117
  102.1 1.3 dynamic-slice
  104.0 0.7 copy_bitcast_fusion.3
  104.8 2.8 convert_reduce_fusion
  107.6 0.9 fusion.32
  108.5 0.2 fusion.46
  108.7 2.8 fusion.7
  111.6 1.7 fusion.55
  113.3 3.1 fusion.25
  116.3 2.0 copy.125
  118.4 2.0 copy.123
  120.4 88.4 %all-reduce.7.cloned.1.call-done = (bf16[1024,2,256]{2,1,0:T(2,128)(2,1)}, bf16[16,128,256]{2,1,0:T(8,128)(2,1)}) async-done(((bf16[1024,2,256]{2,1,0:T(2,128)(2,1)}, bf16[16,128,256]{2,1,0:T(8,128)(2,1)}), (bf16[1024,2,256]{2,1,0:T(2,128)(2,1)}, bf16[16,128,256]{2,1,0:T(8,128)(2,1)})) %all-reduce.7.cloned.1.call-update) | async-done | bytes 2097168
  208.9 2.8 convert_element_type.124
  211.6 1.5 constant_dynamic-slice_fusion
  213.2 93.6 %all-gather.5.cloned.1.call-done = bf16[16,16,128,256]{3,2,1,0:T(8,128)(2,1)} async-done(((bf16[1,16,128,256]{3,2,1,0:T(8,128)(2,1)}), bf16[16,16,128,256]{3,2,1,0:T(8,128)(2,1)}) %all-gather.5.cloned.1.call-update) | async-done | bytes 16777232 | tf_op jit(solution)/shard_map/all_gather | solution.py:125
  306.8 8.9 %reduce_sum.54 = bf16[16,128,256]{2,1,0:T(8,128)(2,1)S(1)} reduce(bf16[16,16,128,256]{3,2,1,0:T(8,128)(2,1)} %all-gather.5.cloned.1.call-done, bf16[]{:T(256)} %constant.26.clone.1), dimensions={0}, to_apply=%region_6.7 | reduce | flops 7864320 | bytes 17825794 | tf_op jit(solution)/shard_map/reduce_sum | solution.py:125
  315.7 1.8 fusion.28
  317.6 1.1 fusion.33
  318.7 1.6 pad_maximum_fusion.1
  320.3 2.1 fusion.12
  322.4 1.4 copy.124
  323.8 42.0 %all-reduce.5.cloned.1.call-done = bf16[256,2,256]{2,0,1:T(8,128)(2,1)} async-done(((bf16[256,2,256]{2,0,1:T(8,128)(2,1)}), bf16[256,2,256]{2,0,1:T(8,128)(2,1)}) %all-reduce.5.cloned.1.call-update) | async-done | bytes 262160 | tf_op jit(solution)/shard_map/psum | solution.py:146
  365.8 0.8 convert_convert_fusion
  366.6 0.7 copy.126
  (69 shorter events, 0.4 us)
Async XLA Ops:
  7.2 97.6 %copy-start = (bf16[256,2048]{1,0:T(8,128)(2,1)S(1)}, bf16[256,2048]{1,0:T(8,128)(2,1)}, u32[]{:S(2)}) copy-start(bf16[256,2048]{1,0:T(8,128)(2,1)} %param.15) | copy-start | bytes 3145732
  7.2 9.8 %copy-start.12 = (bf16[256,2,256]{2,1,0:T(2,128)(2,1)S(1)}, bf16[256,2,256]{2,1,0:T(2,128)(2,1)}, u32[]{:S(2)}) copy-start(bf16[256,2,256]{2,1,0:T(2,128)(2,1)} %param.16) | copy-start | bytes 786436
  7.2 44.2 %all-gather.3.cloned.1.call-start = ((), (), s32[]{:S(2)}) async-start(), calls=%async_computation | async-start | bytes 1114112 | tf_op jit(solution)/shard_map/all_gather | solution.py:36
  7.9 200.9 %all-reduce.7.cloned.1.call-start = ((), (), s32[]{:S(2)}) async-start(), calls=%async_computation.3 | async-start | bytes 4194304
  10.8 8.8 %copy-start.27 = (f32[16,2]{0,1:T(2,128)}, f32[16,2]{0,1:T(2,128)S(1)}, u32[]{:S(2)}) copy-start(f32[16,2]{0,1:T(2,128)S(1)} %slice.29) | copy-start | bytes 388
  12.9 3.9 %copy-start.28 = (f32[256]{0:T(256)}, f32[256]{0:T(256)S(1)}, u32[]{:S(2)}) copy-start(f32[256]{0:T(256)S(1)} %compare_select_fusion) | copy-start | bytes 3076
  18.1 1.5 copy-start.17
  27.6 2.8 copy-start.7
  27.7 0.6 copy-start.15
  62.7 2.5 copy-start.25
  67.0 1.5 copy-start.19
  67.0 3.4 copy-start.5
  68.4 1.9 copy-start.1
  76.2 3.2 copy-start.6
  76.2 3.2 copy-start.20
  76.2 4.6 %copy-start.2 = (bf16[2,4,256,1024]{2,3,1,0:T(8,128)(2,1)S(1)}, bf16[2,4,256,1024]{2,3,1,0:T(8,128)(2,1)}, u32[]{:S(2)}) copy-start(bf16[2,4,256,1024]{2,3,1,0:T(8,128)(2,1)} %copy-done.1) | copy-start | bytes 12582916
  76.2 4.6 %copy-start.10 = (bf16[1024,1,256]{0,2,1:T(8,128)(2,1)S(1)}, bf16[1024,1,256]{0,2,1:T(8,128)(2,1)}, u32[]{:S(2)}) copy-start(bf16[1024,1,256]{0,2,1:T(8,128)(2,1)} %copy.93) | copy-start | bytes 1572868
  80.8 1.8 copy-start.22
  80.8 3.8 %copy-start.8 = (bf16[256,1024]{0,1:T(8,128)(2,1)S(1)}, bf16[256,1024]{0,1:T(8,128)(2,1)}, u32[]{:S(2)}) copy-start(bf16[256,1024]{0,1:T(8,128)(2,1)} %copy.162) | copy-start | bytes 1572868
  82.6 1.9 copy-start.3
  94.6 212.2 %all-gather.5.cloned.1.call-start = ((), (), s32[]{:S(2)}) async-start(), calls=%async_computation.1 | async-start | bytes 17825792 | tf_op jit(solution)/shard_map/all_gather | solution.py:125
  98.2 267.6 %all-reduce.5.cloned.1.call-start = ((), (), s32[]{:S(2)}) async-start(), calls=%async_computation.2 | async-start | bytes 524288 | tf_op jit(solution)/shard_map/psum | solution.py:146
  104.7 3.7 copy-start.13
  104.7 3.9 %copy-start.24 = (pred[256,256]{1,0:T(8,128)(4,1)S(1)}, pred[256,256]{1,0:T(8,128)(4,1)}, u32[]{:S(2)}) copy-start(pred[256,256]{1,0:T(8,128)(4,1)} %copy.97) | copy-start | bytes 196612
  104.7 4.0 %copy-start.26 = (f32[16,256]{1,0:T(8,128)S(1)}, f32[16,256]{1,0:T(8,128)}, u32[]{:S(2)}) copy-start(f32[16,256]{1,0:T(8,128)} %param.17) | copy-start | bytes 49156
  107.5 4.0 %copy-start.16 = (bf16[256,256]{1,0:T(8,128)(2,1)}, bf16[256,256]{1,0:T(8,128)(2,1)S(1)}, u32[]{:S(2)}) copy-start(bf16[256,256]{1,0:T(8,128)(2,1)S(1)} %convert_reduce_fusion) | copy-start | bytes 393220
  108.7 2.8 copy-start.4
  108.7 2.8 copy-start.9
  111.6 1.7 copy-start.21
  111.6 1.7 copy-start.23
  213.2 102.6 %copy-start.11 = (bf16[256,2048]{0,1:T(8,128)(2,1)S(1)}, bf16[256,2048]{0,1:T(8,128)(2,1)}, u32[]{:S(2)}) copy-start(bf16[256,2048]{0,1:T(8,128)(2,1)} %copy.117) | copy-start | bytes 3145732
  213.2 102.6 %copy-start.18 = (f32[256,16]{0,1:T(8,128)S(1)}, f32[256,16]{0,1:T(8,128)}, u32[]{:S(2)}) copy-start(f32[256,16]{0,1:T(8,128)} %copy-done.17) | copy-start | bytes 49156
  213.2 104.4 %copy-start.14 = (bf16[256,1,256]{2,1,0:T(2,128)(2,1)S(1)}, bf16[256,1,256]{2,1,0:T(2,128)(2,1)}, u32[]{:S(2)}) copy-start(bf16[256,1,256]{2,1,0:T(2,128)(2,1)} %get-tuple-element.32) | copy-start | bytes 393220
Sparse Core Ops, SparseCore 0:
  9.9 41.4 all-gather.2
  94.7 114.0 all-reduce.6
  211.3 95.4 all-gather.4
  320.4 45.2 all-reduce.4
